TPU v7x, 32 devices: a whole 2x2x4 slice. The times are simulated.
32 devices in a mesh: grp: 2 (over y), basin: 4 (over z), chain: 2 (over x), mem: 2 (over core).
Axes of the slice: x: 2, y: 2, z: 4, core: 2. Of those that a mesh axis runs over, the one named last changes fastest.
Arguments:
- runoff: float32 [2, 64, 32, 2, 2048], P('mem', 'basin', 'grp', 'chain'), parts along dimension 2, may hold values from 0.002 to 0.02
- directions: int32 [32, 2, 2048], P(('grp', 'basin'), 'chain'), parts along dimension 0, may hold values from 0 to 2
Outputs:
- accumulation: float32 [128, 32, 2, 2048], P('mem', ('grp', 'basin'), 'chain'), parts along dimension 1
There are 2 independent parts, one for each index of `grp`. A program takes and returns all parts, laid end to end along the dimension named above; each array names one. Nothing has to cross between parts.
Inputs may be any that keep to these rules, and one draw needn't show every extreme that they name: `directions`: direction codes of forward three-direction routing: 0 east, 1 north-east, 2 south-east along the flow.
All inputs are finite; a program needn't handle non-finite values.
Results may differ from a plain program's by a relative error of at most 0.0003.
Values sent between devices are 32-bit elements; how exact they have to be, the bound alone decides.
No kernel may reach another device: no remote copies, remote signals or barrier semaphores. Data moves between devices by JAX's collectives and lax.ppermute only.
A program may use at most 128 MiB of HBM per device.

v0:
```python
import jax
import jax.numpy as jnp
from jax import lax
from jax.sharding import PartitionSpec as P

ROWS = 128


def from_behind(value, axis, by):
    count = lax.axis_size(axis)
    pairs = [(i, i + by) for i in range(count) if 0 <= i + by < count]
    return lax.ppermute(value, axis, pairs)


def target_rows(directions):
    cell_count = directions.shape[-1]
    row_ids = jnp.arange(cell_count, dtype=jnp.int32) % ROWS
    offsets = jnp.where(directions == 1, -1, jnp.where(directions == 2, 1, 0)).astype(jnp.int32)
    return jnp.clip(row_ids + offsets, 0, ROWS - 1)


def column_onehot(target_col, kind):
    lane_ids = jnp.arange(ROWS, dtype=jnp.int32)
    return (target_col[..., None] == lane_ids).astype(kind)


def sweep_tile(water_cols, targets, inflow):

    def advance(carried, column_data):
        water_col, target_col = column_data
        summed = water_col + carried
        passed = jnp.einsum(
            "mtj,tji->mti",
            summed,
            column_onehot(target_col, jnp.float32),
            precision=lax.Precision.HIGHEST,
        )
        return (passed, summed)

    return lax.scan(advance, inflow, (jnp.moveaxis(water_cols, 2, 0), jnp.moveaxis(targets, 1, 0)))


def section_matrix(targets):
    tile_count = targets.shape[0]
    start_map = jnp.broadcast_to(jnp.eye(ROWS, dtype=jnp.bfloat16), (tile_count, ROWS, ROWS))

    def chain_step(product, target_col):
        advanced = jnp.einsum(
            "tij,tjk->tik",
            product,
            column_onehot(target_col, jnp.bfloat16),
            preferred_element_type=jnp.float32,
        )
        return (advanced.astype(jnp.bfloat16), None)

    final_map, _ = lax.scan(chain_step, start_map, jnp.moveaxis(targets, 1, 0))
    return final_map.astype(jnp.float32)


def route_chain(water_cols, targets):
    member_count, tile_count = (water_cols.shape[0], water_cols.shape[1])
    no_inflow = jnp.zeros((member_count, tile_count, ROWS), jnp.float32)
    local_flow, _ = sweep_tile(water_cols, targets, no_inflow)
    panel_map = section_matrix(targets)

    def relay_step(counter, state):
        total_out, received = state
        received = from_behind(total_out, "chain", 1)
        total_out = local_flow + jnp.einsum(
            "mtj,tjk->mtk", received, panel_map, precision=lax.Precision.HIGHEST
        )
        return (total_out, received)

    _, inflow = lax.fori_loop(0, lax.axis_size("chain") - 1, relay_step, (local_flow, no_inflow))
    _, columns_out = sweep_tile(water_cols, targets, inflow)
    return columns_out


def local(runoff, directions):
    cell_count = runoff.shape[4]
    col_count = cell_count // ROWS
    regrouped = lax.all_to_all(runoff, "basin", split_axis=2, concat_axis=1, tiled=True)
    member_count, tile_count = (regrouped.shape[1], regrouped.shape[2])
    water_cols = regrouped.reshape(member_count, tile_count, col_count, ROWS)
    targets = target_rows(directions).reshape(tile_count, col_count, ROWS)
    columns_out = route_chain(water_cols, targets)
    return jnp.transpose(columns_out, (1, 2, 0, 3)).reshape(member_count, tile_count, 1, cell_count)


def solution(mesh):
    return jax.shard_map(
        local,
        mesh=mesh,
        in_specs=(P("mem", "basin", "grp", "chain", None), P(("grp", "basin"), "chain", None)),
        out_specs=P("mem", ("grp", "basin"), "chain", None),
        check_vma=False,
    )
```

profile of v0, /device:TPU:0, one launch (start us, length us, event | category | flops | bytes accessed | tf_op | source)
XLA Modules:
  0.0 95.5 jit_solution(6588446960508231606)
XLA Ops:
  0.0 5.1 %copy.10 = f32[1,16,16,1,2048]{4,3,1,0,2:T(1,128)} copy(f32[1,16,16,1,2048]{4,3,2,1,0:T(1,128)} %param.6) | data formatting | bytes 4194304 | tf_op args[0]
  5.1 6.4 %all-to-all-start = ((f32[1,16,16,1,2048]{4,3,1,0,2:T(1,128)}), f32[1,16,16,1,2048]{4,3,1,0,2:T(1,128)S(1)}, u32[]{:S(2)}, u32[]{:S(2)}) async-start(f32[1,16,16,1,2048]{4,3,1,0,2:T(1,128)} %copy.10), calls=%async_computation | async-start | bytes 4194304 | tf_op jit(solution)/shard_map/all_to_all | solution.py:82
  11.7 48.1 %all-to-all-done = f32[1,16,16,1,2048]{4,3,1,0,2:T(1,128)S(1)} async-done(((f32[1,16,16,1,2048]{4,3,1,0,2:T(1,128)}), f32[1,16,16,1,2048]{4,3,1,0,2:T(1,128)S(1)}, u32[]{:S(2)}, u32[]{:S(2)}) %all-to-all-start) | async-done | bytes 2097184 | tf_op jit(solution)/shard_map/all_to_all | solution.py:82
  59.8 0.9 copy.17
  60.9 0.4 copy.18
  61.3 0.7 copy.13
  62.0 6.4 %while.4 = (s32[]{:T(128)}, f32[64,4,128]{2,0,1:T(8,128)S(1)}, s32[16,4,128]{2,1,0:T(4,128)S(1)}, f32[16,64,4,128]{3,1,2,0:T(8,128)S(1)}, s32[]{:T(128)}) while((s32[]{:T(128)}, f32[64,4,128]{2,0,1:T(8,128)S(1)}, s32[16,4,128]{2,1,0:T(4,128)S(1)}, f32[16,64,4,128]{3,1,2,0:T(8,128)S(1)}, s32[]{:T(128)}) %tuple.38), condition=%wide.region_1.2_spmd, body=%wide.region_0.1_spmd.sunk | while | flops 50429952 | bytes 661581 | solution.py:40
  62.0 0.3 convolution_bitcast_fusion.4
  62.4 0.3 convolution_bitcast_fusion.4
  62.8 0.3 convolution_bitcast_fusion.4
  63.2 0.3 convolution_bitcast_fusion.4
  63.6 0.3 convolution_bitcast_fusion.4
  64.0 0.3 convolution_bitcast_fusion.4
  64.4 0.3 convolution_bitcast_fusion.4
  64.8 0.3 convolution_bitcast_fusion.4
  65.2 0.3 convolution_bitcast_fusion.4
  65.6 0.3 convolution_bitcast_fusion.4
  66.0 0.3 convolution_bitcast_fusion.4
  66.4 0.3 convolution_bitcast_fusion.4
  66.8 0.3 convolution_bitcast_fusion.4
  67.2 0.3 convolution_bitcast_fusion.4
  67.6 0.3 convolution_bitcast_fusion.4
  68.0 0.3 convolution_bitcast_fusion.4
  68.4 3.4 %collective-permute-start = (f32[64,4,128]{2,0,1:T(8,128)S(1)}, f32[64,4,128]{2,0,1:T(8,128)S(1)}, u32[]{:S(2)}, u32[]{:S(2)}) collective-permute-start(f32[64,4,128]{2,0,1:T(8,128)S(1)} %get-tuple-element.74), channel_id=1, source_target_pairs={{0,2},{1,3},{4,6},{5,7},{8,10},{9,11},{12,14},{13,15},{16,18},{17,... | collective-permute-start | bytes 393224 | tf_op jit(solution)/shard_map/while/body/eval_jaxpr/ppermute | solution.py:12
  71.8 2.5 %collective-permute-done = f32[64,4,128]{2,0,1:T(8,128)S(1)} collective-permute-done((f32[64,4,128]{2,0,1:T(8,128)S(1)}, f32[64,4,128]{2,0,1:T(8,128)S(1)}, u32[]{:S(2)}, u32[]{:S(2)}) %collective-permute-start) | collective-permute-done | bytes 131104 | tf_op jit(solution)/shard_map/while/body/eval_jaxpr/ppermute | solution.py:12
  74.3 17.1 %while.5 = (s32[]{:T(128)}, f32[64,4,128]{2,0,1:T(8,128)S(1)}, f32[16,64,4,128]{3,1,2,0:T(8,128)}, s32[16,4,128]{2,1,0:T(4,128)S(1)}, f32[16,64,4,128]{3,1,2,0:T(8,128)S(1)}, /*index=5*/s32[]{:T(128)}) while((s32[]{:T(128)}, f32[64,4,128]{2,0,1:T(8,128)S(1)}, f32[16,64,4,128]{3,1,2,0:T(8,128)}, s32[16,4,128]{2,1,0:T(4,128)S(1)}, ...), condition=%wide.region_3.4_spmd, body=%wide.region_2.3_spmd.sunk | while | flops 50462720 | bytes 1054809 | solution.py:40
  74.3 0.7 bitcast_dynamic-update-slice_fusion.2
  75.0 0.3 convolution_bitcast_fusion.5
  75.4 0.7 bitcast_dynamic-update-slice_fusion.2
  76.5 0.7 bitcast_dynamic-update-slice_fusion.2
  77.5 0.7 bitcast_dynamic-update-slice_fusion.2
  78.6 0.7 bitcast_dynamic-update-slice_fusion.2
  79.3 0.3 convolution_bitcast_fusion.5
  79.7 0.7 bitcast_dynamic-update-slice_fusion.2
  80.7 0.7 bitcast_dynamic-update-slice_fusion.2
  81.4 0.3 convolution_bitcast_fusion.5
  81.8 0.7 bitcast_dynamic-update-slice_fusion.2
  82.9 0.7 bitcast_dynamic-update-slice_fusion.2
  83.5 0.3 convolution_bitcast_fusion.5
  83.9 0.7 bitcast_dynamic-update-slice_fusion.2
  85.0 0.7 bitcast_dynamic-update-slice_fusion.2
  86.1 0.7 bitcast_dynamic-update-slice_fusion.2
  87.1 0.7 bitcast_dynamic-update-slice_fusion.2
  88.2 0.7 bitcast_dynamic-update-slice_fusion.2
  89.3 0.7 bitcast_dynamic-update-slice_fusion.2
  90.3 0.7 bitcast_dynamic-update-slice_fusion.2
  91.0 0.3 convolution_bitcast_fusion.5
  91.4 4.1 %copy.16 = f32[64,4,16,128]{3,2,1,0:T(8,128)} copy(f32[64,4,16,128]{3,0,1,2:T(8,128)} %bitcast.53) | data formatting | bytes 4194304 | tf_op jit(solution)/shard_map/transpose | solution.py:87
  (83 shorter events, 4.7 us)
Async XLA Ops:
  5.1 6.5 %copy-start = (s32[4,1,2048]{2,1,0:T(1,128)S(1)}, s32[4,1,2048]{2,1,0:T(1,128)}, u32[]{:S(2)}) copy-start(s32[4,1,2048]{2,1,0:T(1,128)} %param.7) | copy-start | bytes 98308
  5.1 54.6 %all-to-all-start = ((f32[1,16,16,1,2048]{4,3,1,0,2:T(1,128)}), f32[1,16,16,1,2048]{4,3,1,0,2:T(1,128)S(1)}, u32[]{:S(2)}, u32[]{:S(2)}) async-start(f32[1,16,16,1,2048]{4,3,1,0,2:T(1,128)} %copy.10), calls=%async_computation | async-start | bytes 4194304 | tf_op jit(solution)/shard_map/all_to_all | solution.py:82
  68.4 5.9 %collective-permute-start = (f32[64,4,128]{2,0,1:T(8,128)S(1)}, f32[64,4,128]{2,0,1:T(8,128)S(1)}, u32[]{:S(2)}, u32[]{:S(2)}) collective-permute-start(f32[64,4,128]{2,0,1:T(8,128)S(1)} %get-tuple-element.74), channel_id=1, source_target_pairs={{0,2},{1,3},{4,6},{5,7},{8,10},{9,11},{12,14},{13,15},{16,18},{17,... | collective-permute-start | bytes 393224 | tf_op jit(solution)/shard_map/while/body/eval_jaxpr/ppermute | solution.py:12
where the time goes:
time: 95.8 us; the launch traced here: 95.5 us
  waiting for transfers between devices  50.6 us (53%)
  local copies, waits for them, and re-layouts  12.1 us (13%)
  matrix products  10.9 us (11%)
  other arithmetic  10.8 us (11%)
  starting transfers between devices  9.85 us (10%)
  loops' own time  1.22 us (1%)
    all_to_all x1, waiting for transfers between devices, local(): lax.all_to_all(runoff, 'basin', split_axis=2, concat_axis=1, tiled=True)  48.1 us
    dot_general x32, matrix products, advance(): jnp.einsum('mtj,tji->mti', summed, column_onehot(target_col, jnp.float32)...  10.9 us
    dynamic_update_slice x16, other arithmetic, sweep_tile(): lax.scan(advance, inflow, (jnp.moveaxis(water_cols, 2, 0), jnp.moveaxis(t...  10.7 us
    all_to_all x1, starting transfers between devices, local(): lax.all_to_all(runoff, 'basin', split_axis=2, concat_axis=1, tiled=True)  6.45 us
    unnamed x5, local copies, waits for them, and re-layouts  6.37 us
    transpose x1, local copies, waits for them, and re-layouts, local(): jnp.transpose(columns_out, (1, 2, 0, 3))  4.13 us
    ppermute x1, starting transfers between devices, from_behind(): return lax.ppermute(value, axis, pairs)  3.4 us
    ppermute x1, waiting for transfers between devices, from_behind(): return lax.ppermute(value, axis, pairs)  2.49 us
  transfers between devices with their start and end apart: 2, of which 2 were waited for; matrix products, arithmetic and copies ran while one was open for 0% of the time, Pallas kernels for 0%

commit v1 on v0

--- a/solution.py
+++ b/solution.py
@@ -79,7 +79,10 @@
 def local(runoff, directions):
     cell_count = runoff.shape[4]
     col_count = cell_count // ROWS
-    regrouped = lax.all_to_all(runoff, "basin", split_axis=2, concat_axis=1, tiled=True)
+    regrouped = jnp.concatenate(
+        lax.all_to_all(jnp.stack(jnp.split(runoff, lax.axis_size("basin"), axis=2)), "basin", 0, 0),
+        axis=1,
+    )
     member_count, tile_count = (regrouped.shape[1], regrouped.shape[2])
     water_cols = regrouped.reshape(member_count, tile_count, col_count, ROWS)
     targets = target_rows(directions).reshape(tile_count, col_count, ROWS)

time: 95.8 us -> 130 us (1.36)
  matrix products: 10.9 us -> 40 us
  other arithmetic: 10.8 us -> 18.3 us
  local copies, waits for them, and re-layouts: 12.1 us -> 9.2 us
    dot_general x32, matrix products: 10.9 us -> 40 us  [advance(): jnp.einsum('mtj,tji->mti', summed, column_onehot(target_col, jnp.float32)...]
    unnamed x5 -> x2, local copies, waits for them, and re-layouts: 6.37 us -> 0.01 us
    dynamic_update_slice x16, other arithmetic: 10.7 us -> 14.9 us  [sweep_tile(): lax.scan(advance, inflow, (jnp.moveaxis(water_cols, 2, 0), jnp.moveaxis(t...]
    another operation x0 -> x1, local copies, waits for them, and re-layouts: none -> 3.44 us  [local(): jnp.stack(jnp.split(runoff, lax.axis_size('basin'), axis=2))]
    another operation x0 -> x1, other arithmetic: none -> 3.24 us  [local(): jnp.stack(jnp.split(runoff, lax.axis_size('basin'), axis=2))]
    while x2, local copies, waits for them, and re-layouts: 0.69 us -> 2.55 us  [sweep_tile(): lax.scan(advance, inflow, (jnp.moveaxis(water_cols, 2, 0), jnp.moveaxis(t...]
    transpose x1, local copies, waits for them, and re-layouts: 4.13 us -> 2.54 us  [local(): jnp.transpose(columns_out, (1, 2, 0, 3))]
where the time goes in v1:
time: 130 us; the launch traced here: 129 us
  waiting for transfers between devices  50.6 us (39%)
  matrix products  40 us (31%)
  other arithmetic  18.3 us (14%)
  starting transfers between devices  9.85 us (8%)
  local copies, waits for them, and re-layouts  9.2 us (7%)
    all_to_all x1, waiting for transfers between devices, local(): lax.all_to_all(jnp.stack(jnp.split(runoff, lax.axis_size('basin'), axis=2...  48.1 us
    dot_general x32, matrix products, advance(): jnp.einsum('mtj,tji->mti', summed, column_onehot(target_col, jnp.float32)...  40 us
    dynamic_update_slice x16, other arithmetic, sweep_tile(): lax.scan(advance, inflow, (jnp.moveaxis(water_cols, 2, 0), jnp.moveaxis(t...  14.9 us
    all_to_all x1, starting transfers between devices, local(): lax.all_to_all(jnp.stack(jnp.split(runoff, lax.axis_size('basin'), axis=2...  6.45 us
    another operation x1, local copies, waits for them, and re-layouts, local(): jnp.stack(jnp.split(runoff, lax.axis_size('basin'), axis=2))  3.44 us
    ppermute x1, starting transfers between devices, from_behind(): return lax.ppermute(value, axis, pairs)  3.4 us
    another operation x1, other arithmetic, local(): jnp.stack(jnp.split(runoff, lax.axis_size('basin'), axis=2))  3.24 us
  transfers between devices with their start and end apart: 2, of which 2 were waited for; matrix products, arithmetic and copies ran while one was open for 0% of the time, Pallas kernels for 0%

profile of v1, /device:TPU:0, one launch (start us, length us, event | category | flops | bytes accessed | tf_op | source)
XLA Modules:
  0.0 129.1 jit_solution(16076739067042900065)
XLA Ops:
  0.0 3.4 %slice_bitcast_fusion.3 = (f32[1,1,16,4,1,2048]{5,4,3,2,1,0:T(1,128)S(1)}, f32[1,1,16,4,1,2048]{5,4,3,2,1,0:T(1,128)S(1)}, f32[1,1,16,4,1,2048]{5,4,3,2,1,0:T(1,128)S(1)}, f32[1,1,16,4,1,2048]{5,4,3,2,1,0:T(1,128)S(1)}) fusion(f32[1,16,16,1,2048]{4,3,2,1,0:T(1,128)} %param.6), kind=kLoop, calls=%fused_computation.18 | loop fusion | bytes 4194304 | tf_op jit(solution)/shard_map/stack | solution.py:83
  3.5 3.2 %pad_maximum_fusion = f32[4,1,16,4,1,2048]{5,4,3,2,1,0:T(1,128)} fusion(f32[1,1,16,4,1,2048]{5,4,3,2,1,0:T(1,128)S(1)} %get-tuple-element.105, f32[1,1,16,4,1,2048]{5,4,3,2,1,0:T(1,128)S(1)} %get-tuple-element.106, f32[1,1,16,4,1,2048]{5,4,3,2,1,0:T(1,128)S(1)} %get-tuple-element.104, f32[1,1,16,4,1,2048]{5,4,3,2,1,0:T(1,128)S(1)} %get-tuple-element.103), kind=kLoop, calls=%fused_computation.14 | loop fusion | flops 1572864 | bytes 4194304 | tf_op jit(solution)/shard_map/stack | solution.py:83
  6.7 6.4 %all-to-all-start = ((f32[4,1,16,4,1,2048]{5,4,3,2,1,0:T(1,128)}), f32[4,1,16,4,1,2048]{5,4,3,2,1,0:T(1,128)S(1)}, u32[]{:S(2)}, u32[]{:S(2)}) async-start(f32[4,1,16,4,1,2048]{5,4,3,2,1,0:T(1,128)} %pad_maximum_fusion), calls=%async_computation | async-start | bytes 4194304 | tf_op jit(solution)/shard_map/all_to_all | solution.py:83
  13.3 48.1 %all-to-all-done = f32[4,1,16,4,1,2048]{5,4,3,2,1,0:T(1,128)S(1)} async-done(((f32[4,1,16,4,1,2048]{5,4,3,2,1,0:T(1,128)}), f32[4,1,16,4,1,2048]{5,4,3,2,1,0:T(1,128)S(1)}, u32[]{:S(2)}, u32[]{:S(2)}) %all-to-all-start) | async-done | bytes 2097184 | tf_op jit(solution)/shard_map/all_to_all | solution.py:83
  61.3 2.5 %copy.6 = f32[16,64,4,128]{3,1,2,0:T(8,128)} copy(f32[16,64,4,128]{3,0,2,1:T(8,128)S(1)} %bitcast.52) | data formatting | bytes 4194304 | tf_op jit(solution)/shard_map/while | solution.py:40
  63.9 20.9 %while.4 = (s32[]{:T(128)}, f32[64,4,128]{2,0,1:T(8,128)S(1)}, s32[16,4,128]{2,1,0:T(4,128)S(1)}, f32[16,64,4,128]{3,1,2,0:T(8,128)}, s32[]{:T(128)}) while((s32[]{:T(128)}, f32[64,4,128]{2,0,1:T(8,128)S(1)}, s32[16,4,128]{2,1,0:T(4,128)S(1)}, f32[16,64,4,128]{3,1,2,0:T(8,128)}, s32[]{:T(128)}) %tuple.39), condition=%wide.region_1.2_spmd, body=%wide.region_0.1_spmd.sunk | while | flops 50429952 | bytes 661581 | solution.py:40
  63.9 1.2 convolution_bitcast_fusion.4
  65.2 1.2 convolution_bitcast_fusion.4
  66.6 1.2 convolution_bitcast_fusion.4
  67.9 1.2 convolution_bitcast_fusion.4
  69.2 1.2 convolution_bitcast_fusion.4
  70.5 1.2 convolution_bitcast_fusion.4
  71.8 1.2 convolution_bitcast_fusion.4
  73.1 1.2 convolution_bitcast_fusion.4
  74.4 1.2 convolution_bitcast_fusion.4
  75.7 1.2 convolution_bitcast_fusion.4
  77.0 1.2 convolution_bitcast_fusion.4
  78.3 1.2 convolution_bitcast_fusion.4
  79.6 1.2 convolution_bitcast_fusion.4
  81.0 1.2 convolution_bitcast_fusion.4
  82.3 1.2 convolution_bitcast_fusion.4
  83.6 1.2 convolution_bitcast_fusion.4
  84.8 3.4 %collective-permute-start = (f32[64,4,128]{2,0,1:T(8,128)S(1)}, f32[64,4,128]{2,0,1:T(8,128)S(1)}, u32[]{:S(2)}, u32[]{:S(2)}) collective-permute-start(f32[64,4,128]{2,0,1:T(8,128)S(1)} %get-tuple-element.74), channel_id=1, source_target_pairs={{0,2},{1,3},{4,6},{5,7},{8,10},{9,11},{12,14},{13,15},{16,18},{17,... | collective-permute-start | bytes 393224 | tf_op jit(solution)/shard_map/while/body/eval_jaxpr/ppermute | solution.py:12
  88.3 2.5 %collective-permute-done = f32[64,4,128]{2,0,1:T(8,128)S(1)} collective-permute-done((f32[64,4,128]{2,0,1:T(8,128)S(1)}, f32[64,4,128]{2,0,1:T(8,128)S(1)}, u32[]{:S(2)}, u32[]{:S(2)}) %collective-permute-start) | collective-permute-done | bytes 131104 | tf_op jit(solution)/shard_map/while/body/eval_jaxpr/ppermute | solution.py:12
  90.7 35.8 %while.5 = (s32[]{:T(128)}, f32[64,4,128]{2,0,1:T(8,128)S(1)}, f32[16,64,4,128]{3,1,2,0:T(8,128)S(1)}, s32[16,4,128]{2,1,0:T(4,128)S(1)}, f32[16,64,4,128]{3,1,2,0:T(8,128)}, /*index=5*/s32[]{:T(128)}) while((s32[]{:T(128)}, f32[64,4,128]{2,0,1:T(8,128)S(1)}, f32[16,64,4,128]{3,1,2,0:T(8,128)S(1)}, s32[16,4,128]{2,1,0:T(4,128)S(1)}, ...), condition=%wide.region_3.4_spmd, body=%wide.region_2.3_spmd.sunk | while | flops 50462720 | bytes 1054809 | solution.py:40
  90.8 0.9 bitcast_dynamic-update-slice_fusion.2
  91.7 1.2 convolution_bitcast_fusion.5
  93.0 0.9 bitcast_dynamic-update-slice_fusion.2
  93.9 1.2 convolution_bitcast_fusion.5
  95.3 0.9 bitcast_dynamic-update-slice_fusion.2
  96.2 1.2 convolution_bitcast_fusion.5
  98.4 1.2 convolution_bitcast_fusion.5
  99.7 0.9 bitcast_dynamic-update-slice_fusion.2
  100.7 1.2 convolution_bitcast_fusion.5
  102.0 0.9 bitcast_dynamic-update-slice_fusion.2
  102.9 1.2 convolution_bitcast_fusion.5
  105.2 1.2 convolution_bitcast_fusion.5
  106.5 0.9 bitcast_dynamic-update-slice_fusion.2
  107.4 1.2 convolution_bitcast_fusion.5
  109.6 1.2 convolution_bitcast_fusion.5
  111.9 1.2 convolution_bitcast_fusion.5
  114.1 1.2 convolution_bitcast_fusion.5
  116.4 1.2 convolution_bitcast_fusion.5
  118.6 1.2 convolution_bitcast_fusion.5
  120.8 1.2 convolution_bitcast_fusion.5
  123.1 1.2 convolution_bitcast_fusion.5
  125.3 1.2 convolution_bitcast_fusion.5
  126.6 2.5 %copy.9 = f32[64,4,16,128]{3,2,1,0:T(8,128)} copy(f32[64,4,16,128]{3,0,1,2:T(8,128)S(1)} %bitcast.53) | data formatting | bytes 4194304 | tf_op jit(solution)/shard_map/transpose | solution.py:90
  (81 shorter events, 10.1 us)
Async XLA Ops:
  6.7 6.5 %copy-start = (s32[4,1,2048]{2,1,0:T(1,128)S(1)}, s32[4,1,2048]{2,1,0:T(1,128)}, u32[]{:S(2)}) copy-start(s32[4,1,2048]{2,1,0:T(1,128)} %param.7) | copy-start | bytes 98308
  6.7 54.6 %all-to-all-start = ((f32[4,1,16,4,1,2048]{5,4,3,2,1,0:T(1,128)}), f32[4,1,16,4,1,2048]{5,4,3,2,1,0:T(1,128)S(1)}, u32[]{:S(2)}, u32[]{:S(2)}) async-start(f32[4,1,16,4,1,2048]{5,4,3,2,1,0:T(1,128)} %pad_maximum_fusion), calls=%async_computation | async-start | bytes 4194304 | tf_op jit(solution)/shard_map/all_to_all | solution.py:83
  84.8 5.9 %collective-permute-start = (f32[64,4,128]{2,0,1:T(8,128)S(1)}, f32[64,4,128]{2,0,1:T(8,128)S(1)}, u32[]{:S(2)}, u32[]{:S(2)}) collective-permute-start(f32[64,4,128]{2,0,1:T(8,128)S(1)} %get-tuple-element.74), channel_id=1, source_target_pairs={{0,2},{1,3},{4,6},{5,7},{8,10},{9,11},{12,14},{13,15},{16,18},{17,... | collective-permute-start | bytes 393224 | tf_op jit(solution)/shard_map/while/body/eval_jaxpr/ppermute | solution.py:12
